TPU v7x, 512 devices: a whole 4x8x8 slice. The times are simulated.
512 devices in a mesh: leaf: 128 (over z, y, core), sep: 4 (over x).
Axes of the slice: x: 4, y: 8, z: 8, core: 2. Of those that a mesh axis runs over, the one named last changes fastest.
Arguments:
- leaf_source: float32 [128, 640, 256], P('leaf', 'sep'), may hold values from -6 to 6
- leaf_inverse: float32 [128, 640, 640], P('leaf', 'sep'), as said below
- leaf_update: float32 [128, 896, 640], P('leaf', None, 'sep'), as said below
- row_lists: int32 [128, 896], P('leaf'), may hold values from 0 to 255
- row_counts: int32 [128, 7], P('leaf'), may hold values from 1 to 128, as said below
- separator_source: float32 [128, 256, 256], P('leaf', 'sep'), may hold values from -6 to 6
- separator_inverse: float32 [128, 256, 256], P('leaf'), as said below
- separator_coupling: float32 [128, 256, 256], P('leaf'), may hold values from -0.1875 to 0.1875
Outputs:
- leaf_solution: float32 [128, 640, 256], P('leaf', 'sep')
- separator_solution: float32 [128, 256, 256], P('leaf', 'sep')
Inputs may be any that keep to these rules, and one draw needn't show every extreme that they name: `leaf_inverse`: each leaf's block is lower triangular, zero above the diagonal, with diagonal entries between 0.6 and 1.4. `separator_inverse`: each block is lower triangular, zero above the diagonal, with diagonal entries between 0.6 and 1.4. `leaf_update`: row r of a leaf's block belongs to the leaf's ancestor of level 1 + r // 128. `row_lists`: entry r names a row of the leaf's ancestor of level 1 + r // 128. `row_counts`: at every level some leaf has 128 live rows.
All inputs are finite; a program needn't handle non-finite values.
Results may differ from a plain program's by a relative error of at most 0.00011.
Values sent between devices are 32-bit elements; how exact they have to be, the bound alone decides.
A program may use at most 64 MiB of HBM per device.

v0:
```python
import jax
import jax.numpy as jnp
from jax import lax
from jax.sharding import PartitionSpec as P

highest = lax.Precision.HIGHEST


def passed_along(x, axis, by):
    peers = lax.axis_size(axis)
    pairs = [(i, i + by) for i in range(peers) if 0 <= i + by < peers]
    return lax.ppermute(x, axis, pairs)


def product(matrix, operand):
    return jnp.dot(matrix, operand, precision=highest, preferred_element_type=jnp.float32)


def product_first(matrix, operand):
    return lax.dot_general(
        matrix,
        operand,
        (((0,), (0,)), ((), ())),
        precision=highest,
        preferred_element_type=jnp.float32,
    )


def tree_pass(payload, offset):
    return passed_along(payload, "leaf", offset)


def sep_rows(payload):
    return lax.all_gather(payload, "sep", axis=0, tiled=True)


def per_device(
    leaf_source,
    leaf_inverse,
    leaf_update,
    row_lists,
    row_counts,
    separator_source,
    separator_inverse,
    separator_coupling,
):
    depth = row_counts.shape[1]
    leaf_index = lax.axis_index("leaf")
    sep_index = lax.axis_index("sep")
    source = leaf_source[0]
    inverse = leaf_inverse[0]
    update = leaf_update[0]
    quarter = separator_source.shape[1]
    full_rows = separator_inverse.shape[1]
    columns = source.shape[1]
    capacity = row_lists.shape[1] // depth
    first_row = sep_index * quarter
    inverse_block = inverse
    leaf_y = product(inverse_block, lax.all_gather(source, "sep", axis=0, tiled=True))
    slot_index = jnp.arange(depth * capacity) % capacity
    limits = jnp.repeat(row_counts[0], capacity)
    live_rows = (slot_index < limits)[:, None]
    update_terms = jnp.where(live_rows, product(update, leaf_y), 0.0)
    targets = row_lists[0].reshape(depth, capacity)
    picker = (jnp.arange(full_rows)[None, :, None] == targets[:, None, :]).astype(jnp.float32)
    densified = jnp.einsum(
        "kwp,kpn->wkn",
        picker,
        update_terms.reshape(depth, capacity, columns),
        precision=highest,
        preferred_element_type=jnp.float32,
    )
    carried = lax.psum_scatter(densified, "sep", scatter_dimension=0, tiled=True)
    own_source = separator_source[0]
    solver_block = separator_inverse[0]
    coupling = separator_coupling[0]
    coupling_rows = lax.dynamic_slice_in_dim(coupling, first_row, quarter, 0)
    solved_down = jnp.zeros((full_rows, columns), jnp.float32)
    for height in range(1, depth + 1):
        upper_slots = carried[:, height - 1 :]
        stride = 2 ** max(height - 2, 0)
        from_left = tree_pass(upper_slots, stride)
        if height == 1:
            from_right = upper_slots
        else:
            from_right = tree_pass(upper_slots, -stride)
        is_owner = leaf_index % 2**height == 2 ** (height - 1)
        carried = carried.at[:, height - 1 :].set(
            jnp.where(is_owner, from_left + from_right, upper_slots)
        )
        residual_full = sep_rows(own_source - carried[:, height - 1])
        solved = product(solver_block, residual_full)
        solved_down = jnp.where(is_owner, solved, solved_down)
        if height < depth:
            carried = carried.at[:, height].add(
                jnp.where(is_owner, product(coupling_rows, solved), 0.0)
            )
    stacked = jnp.zeros(carried.shape, jnp.float32)
    solution_full = jnp.zeros((full_rows, columns), jnp.float32)
    for height in range(depth, 0, -1):
        is_owner = leaf_index % 2**height == 2 ** (height - 1)
        target = solved_down
        if height < depth:
            stride = 2 ** (height - 1)
            upper_slots = stacked[:, height:]
            from_below = tree_pass(upper_slots, stride)
            from_above = tree_pass(upper_slots, -stride)
            right_child = leaf_index // 2**height % 2 == 1
            received = jnp.where(right_child, from_below, from_above)
            stacked = stacked.at[:, height:].set(jnp.where(is_owner, received, upper_slots))
            parent_full = sep_rows(received[:, 0])
            target = solved_down - product_first(coupling, parent_full)
        solution = product_first(solver_block, target)
        solution_full = jnp.where(is_owner, solution, solution_full)
        own_rows = lax.dynamic_slice_in_dim(solution, first_row, quarter, 0)
        stacked = stacked.at[:, height - 1].set(
            jnp.where(is_owner, own_rows, stacked[:, height - 1])
        )
    from_next = tree_pass(stacked, -1)
    ancestors = jnp.where(leaf_index % 2 == 1, stacked, from_next)
    ancestors_full = sep_rows(ancestors)
    picked = jnp.einsum(
        "kwp,wkn->kpn",
        picker,
        ancestors_full,
        precision=highest,
        preferred_element_type=jnp.float32,
    )
    picked = jnp.where(live_rows, picked.reshape(depth * capacity, columns), 0.0)
    leaf_w = leaf_y - product_first(update, picked)
    inverse_block = inverse
    leaf_x = lax.psum_scatter(
        product_first(inverse_block, leaf_w), "sep", scatter_dimension=0, tiled=True
    )
    separator_rows = lax.dynamic_slice_in_dim(solution_full, first_row, quarter, 0)
    return (leaf_x[None], separator_rows[None])


def solution(mesh):
    placed = (
        P("leaf", "sep", None),
        P("leaf", "sep", None),
        P("leaf", None, "sep"),
        P("leaf", None),
        P("leaf", None),
        P("leaf", "sep", None),
        P("leaf", None, None),
        P("leaf", None, None),
    )
    return jax.shard_map(
        per_device,
        mesh=mesh,
        in_specs=placed,
        out_specs=(P("leaf", "sep", None), P("leaf", "sep", None)),
        check_vma=False,
    )
```

profile of v0, /device:TPU:8, one launch (start us, length us, event | category | flops | bytes accessed | tf_op | source)
XLA Modules:
  0.0 518.3 jit_solution(3606953752508697259)
XLA Ops:
  7.2 13.7 %all-gather = f32[1,640,256]{2,1,0:T(8,128)S(1)} all-gather(f32[1,160,256]{2,1,0:T(8,128)} %param.62), channel_id=2, replica_groups=mesh['leaf'=128,'sep'=4] {'sep'}, dimensions={1}, use_global_device_ids=true | all-gather | bytes 819200 | tf_op jit(solution)/shard_map/all_gather | solution.py:59
  21.7 1.6 fusion.8
  25.8 2.0 copy.66
  27.9 39.7 %reduce-scatter.5.cloned.1.call-done = f32[64,7,256]{2,1,0:T(8,128)} async-done(((f32[256,7,256]{2,1,0:T(8,128)}), f32[64,7,256]{2,1,0:T(8,128)}) %reduce-scatter.5.cloned.1.call-update) | async-done | bytes 458768 | tf_op jit(solution)/shard_map/reduce_scatter | solution.py:73
  68.8 1.9 collective-permute-start
  70.7 7.9 %collective-permute-done = f32[64,7,256]{2,0,1:T(8,128)S(1)} collective-permute-done((f32[64,7,256]{2,0,1:T(8,128)S(1)}, f32[64,7,256]{2,0,1:T(8,128)S(1)}, u32[]{:S(2)}, u32[]{:S(2)}) %collective-permute-start) | collective-permute-done | bytes 458784 | tf_op jit(solution)/shard_map/ppermute | solution.py:12
  79.8 12.4 %all_gather.46 = f32[256,256]{1,0:T(8,128)S(1)} all-gather(f32[64,256]{1,0:T(8,128)S(1)} %fusion.94), channel_id=1, replica_groups=mesh['leaf'=128,'sep'=4] {'sep'}, dimensions={0}, use_global_device_ids=true | all-gather | bytes 327680 | tf_op jit(solution)/shard_map/all_gather | solution.py:34
  93.2 1.9 collective-permute-start.1
  95.2 3.6 collective-permute-start.2
  98.8 3.5 collective-permute-done.1
  102.3 1.8 collective-permute-done.2
  104.2 12.5 %all_gather.47 = f32[256,256]{1,0:T(8,128)S(1)} all-gather(f32[64,256]{1,0:T(8,128)S(1)} %fusion.92), channel_id=1, replica_groups=mesh['leaf'=128,'sep'=4] {'sep'}, dimensions={0}, use_global_device_ids=true | all-gather | bytes 327680 | tf_op jit(solution)/shard_map/all_gather | solution.py:34
  117.8 3.4 collective-permute-start.3
  121.2 2.5 collective-permute-start.4
  123.7 4.8 collective-permute-done.3
  128.5 4.6 collective-permute-done.4
  133.2 12.3 %all_gather.48 = f32[256,256]{1,0:T(8,128)S(1)} all-gather(f32[64,256]{1,0:T(8,128)S(1)} %fusion.90), channel_id=1, replica_groups=mesh['leaf'=128,'sep'=4] {'sep'}, dimensions={0}, use_global_device_ids=true | all-gather | bytes 327680 | tf_op jit(solution)/shard_map/all_gather | solution.py:34
  146.5 6.2 %collective-permute-start.5 = (f32[64,4,256]{2,0,1:T(8,128)S(1)}, f32[64,4,256]{2,0,1:T(8,128)S(1)}, u32[]{:S(2)}, u32[]{:S(2)}) collective-permute-start(f32[64,4,256]{2,0,1:T(8,128)S(1)} %slice.692), channel_id=1, source_target_pairs={{0,16},{4,20},{8,24},{12,28},{16,32},{20,36},{24,40},{28,44},{32,4... | collective-permute-start | bytes 786440 | tf_op jit(solution)/shard_map/ppermute | solution.py:12
  152.7 1.3 collective-permute-start.6
  154.0 5.3 %collective-permute-done.5 = f32[64,4,256]{2,0,1:T(8,128)S(1)} collective-permute-done((f32[64,4,256]{2,0,1:T(8,128)S(1)}, f32[64,4,256]{2,0,1:T(8,128)S(1)}, u32[]{:S(2)}, u32[]{:S(2)}) %collective-permute-start.5) | collective-permute-done | bytes 262176 | tf_op jit(solution)/shard_map/ppermute | solution.py:12
  159.3 5.3 %collective-permute-done.6 = f32[64,4,256]{2,0,1:T(8,128)} collective-permute-done((f32[64,4,256]{2,0,1:T(8,128)S(1)}, f32[64,4,256]{2,0,1:T(8,128)}, u32[]{:S(2)}, u32[]{:S(2)}) %collective-permute-start.6) | collective-permute-done | bytes 262176 | tf_op jit(solution)/shard_map/ppermute | solution.py:12
  165.7 12.3 %all_gather.49 = f32[256,256]{1,0:T(8,128)S(1)} all-gather(f32[64,256]{1,0:T(8,128)S(1)} %fusion.88), channel_id=1, replica_groups=mesh['leaf'=128,'sep'=4] {'sep'}, dimensions={0}, use_global_device_ids=true | all-gather | bytes 327680 | tf_op jit(solution)/shard_map/all_gather | solution.py:34
  178.9 3.6 collective-permute-start.7
  182.6 1.3 collective-permute-start.8
  183.9 3.3 collective-permute-done.7
  187.2 12.7 %collective-permute-done.8 = f32[64,3,256]{2,0,1:T(8,128)S(1)} collective-permute-done((f32[64,3,256]{2,0,1:T(8,128)S(1)}, f32[64,3,256]{2,0,1:T(8,128)S(1)}, u32[]{:S(2)}, u32[]{:S(2)}) %collective-permute-start.8) | collective-permute-done | bytes 196640 | tf_op jit(solution)/shard_map/ppermute | solution.py:12
  199.9 12.3 %all_gather.50 = f32[256,256]{1,0:T(8,128)S(1)} all-gather(f32[64,256]{1,0:T(8,128)S(1)} %fusion.86), channel_id=1, replica_groups=mesh['leaf'=128,'sep'=4] {'sep'}, dimensions={0}, use_global_device_ids=true | all-gather | bytes 327680 | tf_op jit(solution)/shard_map/all_gather | solution.py:34
  213.2 4.5 collective-permute-start.9
  217.7 1.3 collective-permute-start.10
  220.2 4.7 collective-permute-done.10
  225.8 12.3 %all_gather.51 = f32[256,256]{1,0:T(8,128)S(1)} all-gather(f32[64,256]{1,0:T(8,128)S(1)} %fusion.85), channel_id=1, replica_groups=mesh['leaf'=128,'sep'=4] {'sep'}, dimensions={0}, use_global_device_ids=true | all-gather | bytes 327680 | tf_op jit(solution)/shard_map/all_gather | solution.py:34
  239.0 3.7 collective-permute-start.11
  242.7 1.3 collective-permute-start.12
  244.6 5.2 collective-permute-done.12
  249.8 12.4 %all_gather.52 = f32[256,256]{1,0:T(8,128)S(1)} all-gather(f32[64,256]{1,0:T(8,128)S(1)} %bitcast_subtract_fusion), channel_id=1, replica_groups=mesh['leaf'=128,'sep'=4] {'sep'}, dimensions={0}, use_global_device_ids=true | all-gather | bytes 327680 | tf_op jit(solution)/shard_map/all_gather | solution.py:34
  263.5 4.7 collective-permute-start.13
  270.1 5.2 collective-permute-done.14
  275.3 12.7 %all-gather.1 = f32[256,1,256]{2,1,0:T(1,128)S(1)} all-gather(f32[64,1,256]{2,1,0:T(1,128)S(1)} %copy.70), channel_id=3, replica_groups=mesh['leaf'=128,'sep'=4] {'sep'}, dimensions={0}, use_global_device_ids=true | all-gather | bytes 327680 | tf_op jit(solution)/shard_map/all_gather | solution.py:34
  289.3 3.8 collective-permute-start.15
  295.6 4.4 collective-permute-done.16
  300.1 12.3 %all-gather.2 = f32[256,1,256]{2,1,0:T(1,128)S(1)} all-gather(f32[64,1,256]{2,1,0:T(1,128)S(1)} %copy.71), channel_id=4, replica_groups=mesh['leaf'=128,'sep'=4] {'sep'}, dimensions={0}, use_global_device_ids=true | all-gather | bytes 327680 | tf_op jit(solution)/shard_map/all_gather | solution.py:34
  313.6 6.9 %collective-permute-start.17 = (f32[64,3,256]{2,0,1:T(8,128)S(1)}, f32[64,3,256]{2,0,1:T(8,128)S(1)}, u32[]{:S(2)}, u32[]{:S(2)}) collective-permute-start(f32[64,3,256]{2,0,1:T(8,128)S(1)} %slice.705), channel_id=1, source_target_pairs={{0,32},{4,36},{8,40},{12,44},{16,48},{20,52},{24,56},{28,60},{32,6... | collective-permute-start | bytes 589832 | tf_op jit(solution)/shard_map/ppermute | solution.py:12
  321.9 2.9 collective-permute-done.17
  324.8 12.8 %collective-permute-done.18 = f32[64,3,256]{2,0,1:T(8,128)S(1)} collective-permute-done((f32[64,3,256]{2,0,1:T(8,128)S(1)}, f32[64,3,256]{2,0,1:T(8,128)S(1)}, u32[]{:S(2)}, u32[]{:S(2)}) %collective-permute-start.18) | collective-permute-done | bytes 196640 | tf_op jit(solution)/shard_map/ppermute | solution.py:12
  337.7 12.8 %all-gather.3 = f32[256,1,256]{2,1,0:T(1,128)S(1)} all-gather(f32[64,1,256]{2,1,0:T(1,128)S(1)} %copy.72), channel_id=5, replica_groups=mesh['leaf'=128,'sep'=4] {'sep'}, dimensions={0}, use_global_device_ids=true | all-gather | bytes 327680 | tf_op jit(solution)/shard_map/all_gather | solution.py:34
  352.4 1.3 collective-permute-start.19
  355.1 2.6 collective-permute-done.19
  357.7 10.0 %collective-permute-done.20 = f32[64,4,256]{2,0,1:T(8,128)S(1)} collective-permute-done((f32[64,4,256]{2,0,1:T(8,128)S(1)}, f32[64,4,256]{2,0,1:T(8,128)S(1)}, u32[]{:S(2)}, u32[]{:S(2)}) %collective-permute-start.20) | collective-permute-done | bytes 262176 | tf_op jit(solution)/shard_map/ppermute | solution.py:12
  367.9 12.3 %all-gather.4 = f32[256,1,256]{2,1,0:T(1,128)S(1)} all-gather(f32[64,1,256]{2,1,0:T(1,128)S(1)} %copy.73), channel_id=6, replica_groups=mesh['leaf'=128,'sep'=4] {'sep'}, dimensions={0}, use_global_device_ids=true | all-gather | bytes 327680 | tf_op jit(solution)/shard_map/all_gather | solution.py:34
  382.1 3.9 collective-permute-start.21
  386.0 2.0 collective-permute-start.22
  388.0 3.1 collective-permute-done.21
  391.1 5.2 %collective-permute-done.22 = f32[64,5,256]{2,0,1:T(8,128)S(1)} collective-permute-done((f32[64,5,256]{2,0,1:T(8,128)S(1)}, f32[64,5,256]{2,0,1:T(8,128)S(1)}, u32[]{:S(2)}, u32[]{:S(2)}) %collective-permute-start.22) | collective-permute-done | bytes 327712 | tf_op jit(solution)/shard_map/ppermute | solution.py:12
  396.6 12.3 %all-gather.5 = f32[256,1,256]{2,1,0:T(1,128)S(1)} all-gather(f32[64,1,256]{2,1,0:T(1,128)S(1)} %copy.74), channel_id=7, replica_groups=mesh['leaf'=128,'sep'=4] {'sep'}, dimensions={0}, use_global_device_ids=true | all-gather | bytes 327680 | tf_op jit(solution)/shard_map/all_gather | solution.py:34
  410.7 1.9 collective-permute-start.23
  412.6 3.6 collective-permute-start.24
  416.3 3.5 collective-permute-done.23
  419.8 1.8 collective-permute-done.24
  421.8 12.3 %all-gather.6 = f32[256,1,256]{2,1,0:T(1,128)S(1)} all-gather(f32[64,1,256]{2,1,0:T(1,128)S(1)} %copy.75), channel_id=8, replica_groups=mesh['leaf'=128,'sep'=4] {'sep'}, dimensions={0}, use_global_device_ids=true | all-gather | bytes 327680 | tf_op jit(solution)/shard_map/all_gather | solution.py:34
  435.4 1.9 collective-permute-start.25
  437.3 6.0 %collective-permute-done.25 = f32[64,7,256]{2,0,1:T(8,128)S(1)} collective-permute-done((f32[64,7,256]{2,0,1:T(8,128)S(1)}, f32[64,7,256]{2,0,1:T(8,128)S(1)}, u32[]{:S(2)}, u32[]{:S(2)}) %collective-permute-start.25) | collective-permute-done | bytes 458784 | tf_op jit(solution)/shard_map/ppermute | solution.py:12
  444.5 32.9 %all-gather.9.cloned.1.call-done = f32[256,7,256]{2,0,1:T(8,128)} async-done(((f32[64,7,256]{2,0,1:T(8,128)}), f32[256,7,256]{2,0,1:T(8,128)}) %all-gather.9.cloned.1.call-update) | async-done | bytes 1835024 | tf_op jit(solution)/shard_map/all_gather | solution.py:34
  477.4 2.4 convolution_select_fusion
  484.2 25.8 %reduce-scatter.7.cloned.1.call-done = f32[160,256]{1,0:T(8,128)} async-done(((f32[640,256]{1,0:T(8,128)}), f32[160,256]{1,0:T(8,128)}) %reduce-scatter.7.cloned.1.call-update) | async-done | bytes 163856
  (139 shorter events, 41.4 us)
Async XLA Ops:
  7.2 16.1 %copy-start = (f32[1,896,160]{1,2,0:T(8,128)S(1)}, f32[1,896,160]{1,2,0:T(8,128)}, u32[]{:S(2)}) copy-start(f32[1,896,160]{1,2,0:T(8,128)} %param.64) | copy-start | bytes 1720324
  7.2 60.4 %reduce-scatter.5.cloned.1.call-start = ((), (), s32[]{:S(2)}) async-start(), calls=%async_computation.2 | async-start | bytes 2621440 | tf_op jit(solution)/shard_map/reduce_scatter | solution.py:73
  23.3 1.4 copy-start.10
  24.7 3.1 copy-start.8
  27.8 52.0 %copy-start.3 = (f32[1,64,256]{2,1,0:T(8,128)S(1)}, f32[1,64,256]{2,1,0:T(8,128)}, u32[]{:S(2)}) copy-start(f32[1,64,256]{2,1,0:T(8,128)} %param.67) | copy-start | bytes 196612
  27.8 64.4 %copy-start.1 = (f32[1,256,256]{2,1,0:T(8,128)S(1)}, f32[1,256,256]{2,1,0:T(8,128)}, u32[]{:S(2)}) copy-start(f32[1,256,256]{2,1,0:T(8,128)} %param.68) | copy-start | bytes 786436
  27.8 65.0 %copy-start.2 = (f32[1,256,256]{2,1,0:T(8,128)S(1)}, f32[1,256,256]{2,1,0:T(8,128)}, u32[]{:S(2)}) copy-start(f32[1,256,256]{2,1,0:T(8,128)} %param.69) | copy-start | bytes 786436
  27.8 449.6 %all-gather.9.cloned.1.call-start = ((), (), s32[]{:S(2)}) async-start(), calls=%async_computation.3 | async-start | bytes 2293760 | tf_op jit(solution)/shard_map/all_gather | solution.py:34
  68.8 9.8 %collective-permute-start = (f32[64,7,256]{2,0,1:T(8,128)S(1)}, f32[64,7,256]{2,0,1:T(8,128)S(1)}, u32[]{:S(2)}, u32[]{:S(2)}) collective-permute-start(f32[64,7,256]{2,0,1:T(8,128)S(1)} %copy.67), channel_id=1, source_target_pairs={{0,4},{4,8},{8,12},{12,16},{16,20},{20,24},{24,28},{28,32},{32,36}... | collective-permute-start | bytes 1376264 | tf_op jit(solution)/shard_map/ppermute | solution.py:12
  93.2 9.1 %collective-permute-start.1 = (f32[64,6,256]{2,0,1:T(8,128)S(1)}, f32[64,6,256]{2,0,1:T(8,128)S(1)}, u32[]{:S(2)}, u32[]{:S(2)}) collective-permute-start(f32[64,6,256]{2,0,1:T(8,128)S(1)} %slice.686), channel_id=1, source_target_pairs={{0,4},{4,8},{8,12},{12,16},{16,20},{20,24},{24,28},{28,32},{32,36}... | collective-permute-start | bytes 1179656 | tf_op jit(solution)/shard_map/ppermute | solution.py:12
  95.2 8.9 %collective-permute-start.2 = (f32[64,6,256]{2,0,1:T(8,128)S(1)}, f32[64,6,256]{2,0,1:T(8,128)S(1)}, u32[]{:S(2)}, u32[]{:S(2)}) collective-permute-start(f32[64,6,256]{2,0,1:T(8,128)S(1)} %slice.686), channel_id=1, source_target_pairs={{4,0},{8,4},{12,8},{16,12},{20,16},{24,20},{28,24},{32,28},{36,32}... | collective-permute-start | bytes 1179656 | tf_op jit(solution)/shard_map/ppermute | solution.py:12
  117.8 10.7 %collective-permute-start.3 = (f32[64,5,256]{2,0,1:T(8,128)S(1)}, f32[64,5,256]{2,0,1:T(8,128)S(1)}, u32[]{:S(2)}, u32[]{:S(2)}) collective-permute-start(f32[64,5,256]{2,0,1:T(8,128)S(1)} %slice.689), channel_id=1, source_target_pairs={{0,8},{4,12},{8,16},{12,20},{16,24},{20,28},{24,32},{28,36},{32,40... | collective-permute-start | bytes 983048 | tf_op jit(solution)/shard_map/ppermute | solution.py:12
  121.2 11.9 %collective-permute-start.4 = (f32[64,5,256]{2,0,1:T(8,128)S(1)}, f32[64,5,256]{2,0,1:T(8,128)S(1)}, u32[]{:S(2)}, u32[]{:S(2)}) collective-permute-start(f32[64,5,256]{2,0,1:T(8,128)S(1)} %slice.689), channel_id=1, source_target_pairs={{8,0},{12,4},{16,8},{20,12},{24,16},{28,20},{32,24},{36,28},{40,32... | collective-permute-start | bytes 983048 | tf_op jit(solution)/shard_map/ppermute | solution.py:12
  146.5 12.8 %collective-permute-start.5 = (f32[64,4,256]{2,0,1:T(8,128)S(1)}, f32[64,4,256]{2,0,1:T(8,128)S(1)}, u32[]{:S(2)}, u32[]{:S(2)}) collective-permute-start(f32[64,4,256]{2,0,1:T(8,128)S(1)} %slice.692), channel_id=1, source_target_pairs={{0,16},{4,20},{8,24},{12,28},{16,32},{20,36},{24,40},{28,44},{32,4... | collective-permute-start | bytes 786440 | tf_op jit(solution)/shard_map/ppermute | solution.py:12
  152.7 12.0 %collective-permute-start.6 = (f32[64,4,256]{2,0,1:T(8,128)S(1)}, f32[64,4,256]{2,0,1:T(8,128)}, u32[]{:S(2)}, u32[]{:S(2)}) collective-permute-start(f32[64,4,256]{2,0,1:T(8,128)S(1)} %slice.692), channel_id=1, source_target_pairs={{16,0},{20,4},{24,8},{28,12},{32,16},{36,20},{40,24},{44,28},{48,3... | collective-permute-start | bytes 786440 | tf_op jit(solution)/shard_map/ppermute | solution.py:12
  178.9 8.2 %collective-permute-start.7 = (f32[64,3,256]{2,0,1:T(8,128)S(1)}, f32[64,3,256]{2,0,1:T(8,128)S(1)}, u32[]{:S(2)}, u32[]{:S(2)}) collective-permute-start(f32[64,3,256]{2,0,1:T(8,128)S(1)} %slice.695), channel_id=1, source_target_pairs={{0,32},{4,36},{8,40},{12,44},{16,48},{20,52},{24,56},{28,60},{32,6... | collective-permute-start | bytes 589832 | tf_op jit(solution)/shard_map/ppermute | solution.py:12
  182.6 17.3 %collective-permute-start.8 = (f32[64,3,256]{2,0,1:T(8,128)S(1)}, f32[64,3,256]{2,0,1:T(8,128)S(1)}, u32[]{:S(2)}, u32[]{:S(2)}) collective-permute-start(f32[64,3,256]{2,0,1:T(8,128)S(1)} %slice.695), channel_id=1, source_target_pairs={{32,0},{36,4},{40,8},{44,12},{48,16},{52,20},{56,24},{60,28},{64,3... | collective-permute-start | bytes 589832 | tf_op jit(solution)/shard_map/ppermute | solution.py:12
  213.2 7.0 %collective-permute-start.9 = (f32[64,2,256]{2,0,1:T(8,128)S(1)}, f32[64,2,256]{2,0,1:T(8,128)S(1)}, u32[]{:S(2)}, u32[]{:S(2)}) collective-permute-start(f32[64,2,256]{2,0,1:T(8,128)S(1)} %slice.698), channel_id=1, source_target_pairs={{0,64},{4,68},{8,72},{12,76},{16,80},{20,84},{24,88},{28,92},{32,9... | collective-permute-start | bytes 393224 | tf_op jit(solution)/shard_map/ppermute | solution.py:12
  217.7 7.2 %collective-permute-start.10 = (f32[64,2,256]{2,0,1:T(8,128)S(1)}, f32[64,2,256]{2,0,1:T(8,128)}, u32[]{:S(2)}, u32[]{:S(2)}) collective-permute-start(f32[64,2,256]{2,0,1:T(8,128)S(1)} %slice.698), channel_id=1, source_target_pairs={{64,0},{68,4},{72,8},{76,12},{80,16},{84,20},{88,24},{92,28},{96,3... | collective-permute-start | bytes 393224 | tf_op jit(solution)/shard_map/ppermute | solution.py:12
  239.0 5.6 %collective-permute-start.11 = (f32[64,1,256]{2,0,1:T(8,128)S(1)}, f32[64,1,256]{2,0,1:T(8,128)S(1)}, u32[]{:S(2)}, u32[]{:S(2)}) collective-permute-start(f32[64,1,256]{2,0,1:T(8,128)S(1)} %slice_add_fusion), channel_id=1, source_target_pairs={{0,128},{4,132},{8,136},{12,140},{16,144},{20,148},{24,152},{28,15... | collective-permute-start | bytes 196616 | tf_op jit(solution)/shard_map/ppermute | solution.py:12
  242.7 7.1 %collective-permute-start.12 = (f32[64,1,256]{2,0,1:T(8,128)S(1)}, f32[64,1,256]{2,0,1:T(8,128)S(1)}, u32[]{:S(2)}, u32[]{:S(2)}) collective-permute-start(f32[64,1,256]{2,0,1:T(8,128)S(1)} %slice_add_fusion), channel_id=1, source_target_pairs={{128,0},{132,4},{136,8},{140,12},{144,16},{148,20},{152,24},{156,2... | collective-permute-start | bytes 196616 | tf_op jit(solution)/shard_map/ppermute | solution.py:12
  263.5 6.6 %collective-permute-start.13 = (f32[64,1,256]{2,0,1:T(8,128)S(1)}, f32[64,1,256]{2,0,1:T(8,128)S(1)}, u32[]{:S(2)}, u32[]{:S(2)}) collective-permute-start(f32[64,1,256]{2,0,1:T(8,128)S(1)} %select_bitcast_fusion), channel_id=1, source_target_pairs={{0,128},{4,132},{8,136},{12,140},{16,144},{20,148},{24,152},{28,15... | collective-permute-start | bytes 196616 | tf_op jit(solution)/shard_map/ppermute | solution.py:12
  268.2 7.1 %collective-permute-start.14 = (f32[64,1,256]{2,0,1:T(8,128)S(1)}, f32[64,1,256]{2,0,1:T(8,128)S(1)}, u32[]{:S(2)}, u32[]{:S(2)}) collective-permute-start(f32[64,1,256]{2,0,1:T(8,128)S(1)} %select_bitcast_fusion), channel_id=1, source_target_pairs={{128,0},{132,4},{136,8},{140,12},{144,16},{148,20},{152,24},{156,2... | collective-permute-start | bytes 196616 | tf_op jit(solution)/shard_map/ppermute | solution.py:12
  289.3 6.3 %collective-permute-start.15 = (f32[64,2,256]{2,0,1:T(8,128)S(1)}, f32[64,2,256]{2,0,1:T(8,128)S(1)}, u32[]{:S(2)}, u32[]{:S(2)}) collective-permute-start(f32[64,2,256]{2,0,1:T(8,128)S(1)} %slice.702), channel_id=1, source_target_pairs={{0,64},{4,68},{8,72},{12,76},{16,80},{20,84},{24,88},{28,92},{32,9... | collective-permute-start | bytes 393224 | tf_op jit(solution)/shard_map/ppermute | solution.py:12
  293.1 6.9 %collective-permute-start.16 = (f32[64,2,256]{2,0,1:T(8,128)S(1)}, f32[64,2,256]{2,0,1:T(8,128)S(1)}, u32[]{:S(2)}, u32[]{:S(2)}) collective-permute-start(f32[64,2,256]{2,0,1:T(8,128)S(1)} %slice.702), channel_id=1, source_target_pairs={{64,0},{68,4},{72,8},{76,12},{80,16},{84,20},{88,24},{92,28},{96,3... | collective-permute-start | bytes 393224 | tf_op jit(solution)/shard_map/ppermute | solution.py:12
  313.6 11.1 %collective-permute-start.17 = (f32[64,3,256]{2,0,1:T(8,128)S(1)}, f32[64,3,256]{2,0,1:T(8,128)S(1)}, u32[]{:S(2)}, u32[]{:S(2)}) collective-permute-start(f32[64,3,256]{2,0,1:T(8,128)S(1)} %slice.705), channel_id=1, source_target_pairs={{0,32},{4,36},{8,40},{12,44},{16,48},{20,52},{24,56},{28,60},{32,6... | collective-permute-start | bytes 589832 | tf_op jit(solution)/shard_map/ppermute | solution.py:12
  320.6 17.0 %collective-permute-start.18 = (f32[64,3,256]{2,0,1:T(8,128)S(1)}, f32[64,3,256]{2,0,1:T(8,128)S(1)}, u32[]{:S(2)}, u32[]{:S(2)}) collective-permute-start(f32[64,3,256]{2,0,1:T(8,128)S(1)} %slice.705), channel_id=1, source_target_pairs={{32,0},{36,4},{40,8},{44,12},{48,16},{52,20},{56,24},{60,28},{64,3... | collective-permute-start | bytes 589832 | tf_op jit(solution)/shard_map/ppermute | solution.py:12
  352.4 5.2 %collective-permute-start.19 = (f32[64,4,256]{2,0,1:T(8,128)S(1)}, f32[64,4,256]{2,0,1:T(8,128)S(1)}, u32[]{:S(2)}, u32[]{:S(2)}) collective-permute-start(f32[64,4,256]{2,0,1:T(8,128)S(1)} %slice.708), channel_id=1, source_target_pairs={{0,16},{4,20},{8,24},{12,28},{16,32},{20,36},{24,40},{28,44},{32,4... | collective-permute-start | bytes 786440 | tf_op jit(solution)/shard_map/ppermute | solution.py:12
  353.8 13.9 %collective-permute-start.20 = (f32[64,4,256]{2,0,1:T(8,128)S(1)}, f32[64,4,256]{2,0,1:T(8,128)S(1)}, u32[]{:S(2)}, u32[]{:S(2)}) collective-permute-start(f32[64,4,256]{2,0,1:T(8,128)S(1)} %slice.708), channel_id=1, source_target_pairs={{16,0},{20,4},{24,8},{28,12},{32,16},{36,20},{40,24},{44,28},{48,3... | collective-permute-start | bytes 786440 | tf_op jit(solution)/shard_map/ppermute | solution.py:12
  382.1 9.0 %collective-permute-start.21 = (f32[64,5,256]{2,0,1:T(8,128)S(1)}, f32[64,5,256]{2,0,1:T(8,128)S(1)}, u32[]{:S(2)}, u32[]{:S(2)}) collective-permute-start(f32[64,5,256]{2,0,1:T(8,128)S(1)} %slice.711), channel_id=1, source_target_pairs={{0,8},{4,12},{8,16},{12,20},{16,24},{20,28},{24,32},{28,36},{32,40... | collective-permute-start | bytes 983048 | tf_op jit(solution)/shard_map/ppermute | solution.py:12
  386.0 10.3 %collective-permute-start.22 = (f32[64,5,256]{2,0,1:T(8,128)S(1)}, f32[64,5,256]{2,0,1:T(8,128)S(1)}, u32[]{:S(2)}, u32[]{:S(2)}) collective-permute-start(f32[64,5,256]{2,0,1:T(8,128)S(1)} %slice.711), channel_id=1, source_target_pairs={{8,0},{12,4},{16,8},{20,12},{24,16},{28,20},{32,24},{36,28},{40,32... | collective-permute-start | bytes 983048 | tf_op jit(solution)/shard_map/ppermute | solution.py:12
  410.7 9.1 %collective-permute-start.23 = (f32[64,6,256]{2,0,1:T(8,128)S(1)}, f32[64,6,256]{2,0,1:T(8,128)S(1)}, u32[]{:S(2)}, u32[]{:S(2)}) collective-permute-start(f32[64,6,256]{2,0,1:T(8,128)S(1)} %slice.714), channel_id=1, source_target_pairs={{0,4},{4,8},{8,12},{12,16},{16,20},{20,24},{24,28},{28,32},{32,36}... | collective-permute-start | bytes 1179656 | tf_op jit(solution)/shard_map/ppermute | solution.py:12
  412.6 8.9 %collective-permute-start.24 = (f32[64,6,256]{2,0,1:T(8,128)S(1)}, f32[64,6,256]{2,0,1:T(8,128)S(1)}, u32[]{:S(2)}, u32[]{:S(2)}) collective-permute-start(f32[64,6,256]{2,0,1:T(8,128)S(1)} %slice.714), channel_id=1, source_target_pairs={{4,0},{8,4},{12,8},{16,12},{20,16},{24,20},{28,24},{32,28},{36,32}... | collective-permute-start | bytes 1179656 | tf_op jit(solution)/shard_map/ppermute | solution.py:12
  434.1 10.3 %copy-start.11 = (s32[1,7]{1,0:T(1,128)S(1)}, s32[1,7]{1,0:T(1,128)}, u32[]{:S(2)}) copy-start(s32[1,7]{1,0:T(1,128)} %param.66) | copy-start | bytes 88
  434.1 43.2 %copy-start.9 = (s32[896]{0:T(1024)S(1)}, s32[896]{0:T(1024)}, u32[]{:S(2)}) copy-start(s32[896]{0:T(1024)} %copy-done.8) | copy-start | bytes 10756
  435.4 7.9 %collective-permute-start.25 = (f32[64,7,256]{2,0,1:T(8,128)S(1)}, f32[64,7,256]{2,0,1:T(8,128)S(1)}, u32[]{:S(2)}, u32[]{:S(2)}) collective-permute-start(f32[64,7,256]{2,0,1:T(8,128)S(1)} %get-tuple-element.328), channel_id=1, source_target_pairs={{4,0},{8,4},{12,8},{16,12},{20,16},{24,20},{28,24},{32,28},{36,32}... | collective-permute-start | bytes 1376264 | tf_op jit(solution)/shard_map/ppermute | solution.py:12
  444.2 65.8 %reduce-scatter.7.cloned.1.call-start = ((), (), s32[]{:S(2)}) async-start(), calls=%async_computation.4 | async-start | bytes 819200
  444.5 36.0 %copy-start.4 = (f32[1,160,640]{2,1,0:T(8,128)S(1)}, f32[1,160,640]{2,1,0:T(8,128)}, u32[]{:S(2)}) copy-start(f32[1,160,640]{2,1,0:T(8,128)} %param.63) | copy-start | bytes 1228804
  481.4 1.5 copy-start.5
  481.4 1.6 copy-start.6
  481.4 1.7 copy-start.7
Sparse Core Ops, SparseCore 0:
  27.9 39.6 reduce-scatter.4
  444.3 33.0 all-gather.8
  482.7 27.2 reduce-scatter.6
where the time goes:
time: 519 us; the launch traced here: 518 us
  waiting for transfers between devices  218 us (42%)
  blocking collectives  175 us (34%)
  starting transfers between devices  72.1 us (14%)
  matrix products  21.9 us (4%)
  between operations  15 us (3%)
  local copies, waits for them, and re-layouts  8.57 us (2%)
  other arithmetic  7.86 us (2%)
    all_gather x13, blocking collectives, sep_rows(): return lax.all_gather(payload, 'sep', axis=0, tiled=True)  161 us
    ppermute x26, waiting for transfers between devices, passed_along(): return lax.ppermute(x, axis, pairs)  120 us
    ppermute x26, starting transfers between devices, passed_along(): return lax.ppermute(x, axis, pairs)  71.8 us
    reduce_scatter x1, waiting for transfers between devices, per_device(): lax.psum_scatter(densified, 'sep', scatter_dimension=0, tiled=True)  39.7 us
    all_gather x1, waiting for transfers between devices, sep_rows(): return lax.all_gather(payload, 'sep', axis=0, tiled=True)  32.9 us
    unnamed x4, waiting for transfers between devices  25.8 us
    all_gather x1, blocking collectives, per_device(): lax.all_gather(source, 'sep', axis=0, tiled=True)  13.7 us
  transfers between devices with their start and end apart: 29, of which 29 were waited for; matrix products, arithmetic and copies ran while one was open for 0% of the time, Pallas kernels for 0%

commit v1 on v0

--- a/solution.py
+++ b/solution.py
@@ -31,7 +31,14 @@
 
 
 def sep_rows(payload):
-    return lax.all_gather(payload, "sep", axis=0, tiled=True)
+
+    def get_the_group(u):
+        block_next = tuple((u for _ in range(lax.axis_size("sep"))))
+        reached = jnp.stack(block_next, axis=0)
+        u_next = lax.all_to_all(reached, "sep", 0, 0)
+        return jnp.concatenate(u_next, 0)
+
+    return get_the_group(payload)
 
 
 def per_device(

time: 519 us -> 483 us (0.931)
  blocking collectives: 175 us -> 87 us
  starting transfers between devices: 72.1 us -> 105 us
  waiting for transfers between devices: 218 us -> 230 us
  local copies, waits for them, and re-layouts: 8.57 us -> 14.5 us
    all_gather x13 -> x0, blocking collectives: 161 us -> none  [sep_rows(): return lax.all_gather(payload, 'sep', axis=0, tiled=True)]
    all_to_all x0 -> x8, blocking collectives: none -> 73.2 us  [get_the_group(): u_next = lax.all_to_all(reached, 'sep', 0, 0)]
    all_to_all x0 -> x6, waiting for transfers between devices: none -> 58.4 us  [get_the_group(): u_next = lax.all_to_all(reached, 'sep', 0, 0)]
    all_gather x1 -> x0, waiting for transfers between devices: 32.9 us -> none  [sep_rows(): return lax.all_gather(payload, 'sep', axis=0, tiled=True)]
    all_to_all x0 -> x6, starting transfers between devices: none -> 20.7 us  [get_the_group(): u_next = lax.all_to_all(reached, 'sep', 0, 0)]
    ppermute x26, starting transfers between devices: 71.8 us -> 84.1 us  [passed_along(): return lax.ppermute(x, axis, pairs)]
    ppermute x26, waiting for transfers between devices: 120 us -> 110 us  [passed_along(): return lax.ppermute(x, axis, pairs)]
    another operation x0 -> x19, local copies, waits for them, and re-layouts: none -> 5.27 us  [get_the_group(): reached = jnp.stack(block_next, axis=0)]
  transfers between devices with their start and end apart: 29 -> 34, of which waited for: 29 -> 34; matrix products, arithmetic and copies ran while one was open for 0% -> 0% of each run, Pallas kernels for 0% -> 0%
where the time goes in v1:
time: 483 us; the launch traced here: 481 us
  waiting for transfers between devices  230 us (48%)
  starting transfers between devices  105 us (22%)
  blocking collectives  87 us (18%)
  matrix products  22.5 us (5%)
  between operations  15.4 us (3%)
  local copies, waits for them, and re-layouts  14.5 us (3%)
  other arithmetic  7.11 us (1%)
    ppermute x26, waiting for transfers between devices, passed_along(): return lax.ppermute(x, axis, pairs)  110 us
    ppermute x26, starting transfers between devices, passed_along(): return lax.ppermute(x, axis, pairs)  84.1 us
    all_to_all x8, blocking collectives, get_the_group(): u_next = lax.all_to_all(reached, 'sep', 0, 0)  73.2 us
    all_to_all x6, waiting for transfers between devices, get_the_group(): u_next = lax.all_to_all(reached, 'sep', 0, 0)  58.4 us
    reduce_scatter x1, waiting for transfers between devices, per_device(): lax.psum_scatter(densified, 'sep', scatter_dimension=0, tiled=True)  39.8 us
    unnamed x3, waiting for transfers between devices  21.1 us
    all_to_all x6, starting transfers between devices, get_the_group(): u_next = lax.all_to_all(reached, 'sep', 0, 0)  20.7 us
    all_gather x1, blocking collectives, per_device(): lax.all_gather(source, 'sep', axis=0, tiled=True)  13.7 us
  transfers between devices with their start and end apart: 34, of which 34 were waited for; matrix products, arithmetic and copies ran while one was open for 0% of the time, Pallas kernels for 0%

profile of v1, /device:TPU:8, one launch (start us, length us, event | category | flops | bytes accessed | tf_op | source)
XLA Modules:
  0.0 481.3 jit_solution(7659402302962781347)
XLA Ops:
  7.2 13.7 %all-gather = f32[1,640,256]{2,1,0:T(8,128)S(1)} all-gather(f32[1,160,256]{2,1,0:T(8,128)} %param.62), channel_id=2, replica_groups=mesh['leaf'=128,'sep'=4] {'sep'}, dimensions={1}, use_global_device_ids=true | all-gather | bytes 819200 | tf_op jit(solution)/shard_map/all_gather | solution.py:66
  21.7 1.6 fusion.8
  25.6 2.3 convolution_bitcast_fusion
  27.9 1.9 copy.104
  29.9 39.8 %reduce-scatter.5.cloned.1.call-done = f32[64,7,256]{2,1,0:T(8,128)} async-done(((f32[256,7,256]{2,1,0:T(8,128)}), f32[64,7,256]{2,1,0:T(8,128)}) %reduce-scatter.5.cloned.1.call-update) | async-done | bytes 458768 | tf_op jit(solution)/shard_map/reduce_scatter | solution.py:80
  70.9 2.1 collective-permute-start
  73.0 7.9 %collective-permute-done = f32[64,7,256]{2,0,1:T(8,128)S(1)} collective-permute-done((f32[64,7,256]{2,0,1:T(8,128)S(1)}, f32[64,7,256]{2,0,1:T(8,128)S(1)}, u32[]{:S(2)}, u32[]{:S(2)}) %collective-permute-start) | collective-permute-done | bytes 458784 | tf_op jit(solution)/shard_map/ppermute | solution.py:12
  82.8 3.4 all-to-all-start
  86.2 6.6 %all-to-all-done = f32[4,64,256]{2,1,0:T(8,128)S(1)} async-done(((f32[4,64,256]{2,1,0:T(8,128)}), f32[4,64,256]{2,1,0:T(8,128)S(1)}, u32[]{:S(2)}, u32[]{:S(2)}) %all-to-all-start) | async-done | bytes 262176 | tf_op jit(solution)/shard_map/all_to_all | solution.py:38
  93.9 1.9 collective-permute-start.1
  95.8 3.6 collective-permute-start.2
  99.5 3.5 collective-permute-done.1
  103.0 1.8 collective-permute-done.2
  105.6 3.4 all-to-all-start.1
  109.0 7.3 %all-to-all-done.1 = f32[4,64,256]{2,1,0:T(8,128)S(1)} async-done(((f32[4,64,256]{2,1,0:T(8,128)}), f32[4,64,256]{2,1,0:T(8,128)S(1)}, u32[]{:S(2)}, u32[]{:S(2)}) %all-to-all-start.1) | async-done | bytes 262176 | tf_op jit(solution)/shard_map/all_to_all | solution.py:38
  117.3 2.7 collective-permute-start.3
  120.1 3.1 collective-permute-start.4
  123.2 6.2 %collective-permute-done.3 = f32[64,5,256]{2,0,1:T(8,128)S(1)} collective-permute-done((f32[64,5,256]{2,0,1:T(8,128)S(1)}, f32[64,5,256]{2,0,1:T(8,128)S(1)}, u32[]{:S(2)}, u32[]{:S(2)}) %collective-permute-start.3) | collective-permute-done | bytes 327712 | tf_op jit(solution)/shard_map/ppermute | solution.py:12
  131.4 3.4 all-to-all-start.2
  134.8 7.0 %all-to-all-done.2 = f32[4,64,256]{2,1,0:T(8,128)S(1)} async-done(((f32[4,64,256]{2,1,0:T(8,128)}), f32[4,64,256]{2,1,0:T(8,128)S(1)}, u32[]{:S(2)}, u32[]{:S(2)}) %all-to-all-start.2) | async-done | bytes 262176 | tf_op jit(solution)/shard_map/all_to_all | solution.py:38
  142.8 8.9 %collective-permute-start.5 = (f32[64,4,256]{2,0,1:T(8,128)S(1)}, f32[64,4,256]{2,0,1:T(8,128)S(1)}, u32[]{:S(2)}, u32[]{:S(2)}) collective-permute-start(f32[64,4,256]{2,0,1:T(8,128)S(1)} %slice.692), channel_id=1, source_target_pairs={{0,16},{4,20},{8,24},{12,28},{16,32},{20,36},{24,40},{28,44},{32,4... | collective-permute-start | bytes 786440 | tf_op jit(solution)/shard_map/ppermute | solution.py:12
  153.0 3.8 collective-permute-done.5
  156.8 7.0 %collective-permute-done.6 = f32[64,4,256]{2,0,1:T(8,128)} collective-permute-done((f32[64,4,256]{2,0,1:T(8,128)S(1)}, f32[64,4,256]{2,0,1:T(8,128)}, u32[]{:S(2)}, u32[]{:S(2)}) %collective-permute-start.6) | collective-permute-done | bytes 262176 | tf_op jit(solution)/shard_map/ppermute | solution.py:12
  165.5 3.4 all-to-all-start.3
  169.0 6.6 %all-to-all-done.3 = f32[4,64,256]{2,1,0:T(8,128)S(1)} async-done(((f32[4,64,256]{2,1,0:T(8,128)}), f32[4,64,256]{2,1,0:T(8,128)S(1)}, u32[]{:S(2)}, u32[]{:S(2)}) %all-to-all-start.3) | async-done | bytes 262176 | tf_op jit(solution)/shard_map/all_to_all | solution.py:38
  176.6 6.9 %collective-permute-start.7 = (f32[64,3,256]{2,0,1:T(8,128)S(1)}, f32[64,3,256]{2,0,1:T(8,128)S(1)}, u32[]{:S(2)}, u32[]{:S(2)}) collective-permute-start(f32[64,3,256]{2,0,1:T(8,128)S(1)} %slice.695), channel_id=1, source_target_pairs={{0,32},{4,36},{8,40},{12,44},{16,48},{20,52},{24,56},{28,60},{32,6... | collective-permute-start | bytes 589832 | tf_op jit(solution)/shard_map/ppermute | solution.py:12
  184.8 1.9 collective-permute-done.7
  186.7 14.5 %collective-permute-done.8 = f32[64,3,256]{2,0,1:T(8,128)} collective-permute-done((f32[64,3,256]{2,0,1:T(8,128)S(1)}, f32[64,3,256]{2,0,1:T(8,128)}, u32[]{:S(2)}, u32[]{:S(2)}) %collective-permute-start.8) | collective-permute-done | bytes 196640 | tf_op jit(solution)/shard_map/ppermute | solution.py:12
  202.9 3.4 all-to-all-start.4
  206.4 6.6 %all-to-all-done.4 = f32[4,64,256]{2,1,0:T(8,128)S(1)} async-done(((f32[4,64,256]{2,1,0:T(8,128)}), f32[4,64,256]{2,1,0:T(8,128)S(1)}, u32[]{:S(2)}, u32[]{:S(2)}) %all-to-all-start.4) | async-done | bytes 262176 | tf_op jit(solution)/shard_map/all_to_all | solution.py:38
  215.3 4.6 collective-permute-start.9
  220.8 1.5 collective-permute-done.9
  222.4 9.1 %all_to_all.70 = f32[4,64,256]{2,1,0:T(8,128)S(1)} all-to-all(f32[4,64,256]{2,1,0:T(8,128)S(1)} %stack.99), channel_id=1, replica_groups=mesh['leaf'=128,'sep'=4] {'sep'}, dimensions={0} | all-to-all | bytes 524288 | tf_op jit(solution)/shard_map/all_to_all | solution.py:38
  232.4 5.8 %collective-permute-start.11 = (f32[64,1,256]{2,0,1:T(8,128)S(1)}, f32[64,1,256]{2,0,1:T(8,128)S(1)}, u32[]{:S(2)}, u32[]{:S(2)}) collective-permute-start(f32[64,1,256]{2,0,1:T(8,128)S(1)} %slice_add_fusion), channel_id=1, source_target_pairs={{0,128},{4,132},{8,136},{12,140},{16,144},{20,148},{24,152},{28,15... | collective-permute-start | bytes 196616 | tf_op jit(solution)/shard_map/ppermute | solution.py:12
  240.1 8.5 %collective-permute-done.12 = f32[64,1,256]{2,0,1:T(8,128)S(1)} collective-permute-done((f32[64,1,256]{2,0,1:T(8,128)S(1)}, f32[64,1,256]{2,0,1:T(8,128)S(1)}, u32[]{:S(2)}, u32[]{:S(2)}) %collective-permute-start.12) | collective-permute-done | bytes 65568 | tf_op jit(solution)/shard_map/ppermute | solution.py:12
  248.7 9.1 %all_to_all.71 = f32[4,64,256]{2,1,0:T(8,128)S(1)} all-to-all(f32[4,64,256]{2,1,0:T(8,128)S(1)} %stack.101), channel_id=1, replica_groups=mesh['leaf'=128,'sep'=4] {'sep'}, dimensions={0} | all-to-all | bytes 524288 | tf_op jit(solution)/shard_map/all_to_all | solution.py:38
  259.0 6.0 %collective-permute-start.13 = (f32[64,1,256]{2,0,1:T(8,128)S(1)}, f32[64,1,256]{2,0,1:T(8,128)S(1)}, u32[]{:S(2)}, u32[]{:S(2)}) collective-permute-start(f32[64,1,256]{2,0,1:T(8,128)S(1)} %select_bitcast_fusion), channel_id=1, source_target_pairs={{0,128},{4,132},{8,136},{12,140},{16,144},{20,148},{24,152},{28,15... | collective-permute-start | bytes 196616 | tf_op jit(solution)/shard_map/ppermute | solution.py:12
  266.9 5.2 %collective-permute-done.14 = f32[64,1,256]{2,0,1:T(8,128)S(1)} collective-permute-done((f32[64,1,256]{2,0,1:T(8,128)S(1)}, f32[64,1,256]{2,0,1:T(8,128)S(1)}, u32[]{:S(2)}, u32[]{:S(2)}) %collective-permute-start.14) | collective-permute-done | bytes 65568 | tf_op jit(solution)/shard_map/ppermute | solution.py:12
  272.1 9.1 %all_to_all.72 = f32[4,64,256]{2,1,0:T(8,128)S(1)} all-to-all(f32[4,64,256]{2,1,0:T(8,128)S(1)} %stack.102), channel_id=1, replica_groups=mesh['leaf'=128,'sep'=4] {'sep'}, dimensions={0} | all-to-all | bytes 524288 | tf_op jit(solution)/shard_map/all_to_all | solution.py:38
  286.3 4.6 collective-permute-done.16
  291.1 9.1 %all_to_all.73 = f32[4,64,256]{2,1,0:T(8,128)S(1)} all-to-all(f32[4,64,256]{2,1,0:T(8,128)S(1)} %stack.103), channel_id=1, replica_groups=mesh['leaf'=128,'sep'=4] {'sep'}, dimensions={0} | all-to-all | bytes 524288 | tf_op jit(solution)/shard_map/all_to_all | solution.py:38
  301.4 7.1 %collective-permute-start.17 = (f32[64,3,256]{2,0,1:T(8,128)S(1)}, f32[64,3,256]{2,0,1:T(8,128)S(1)}, u32[]{:S(2)}, u32[]{:S(2)}) collective-permute-start(f32[64,3,256]{2,0,1:T(8,128)S(1)} %slice.705), channel_id=1, source_target_pairs={{0,32},{4,36},{8,40},{12,44},{16,48},{20,52},{24,56},{28,60},{32,6... | collective-permute-start | bytes 589832 | tf_op jit(solution)/shard_map/ppermute | solution.py:12
  309.8 2.4 collective-permute-done.17
  312.2 10.6 %collective-permute-done.18 = f32[64,3,256]{2,0,1:T(8,128)S(1)} collective-permute-done((f32[64,3,256]{2,0,1:T(8,128)S(1)}, f32[64,3,256]{2,0,1:T(8,128)S(1)}, u32[]{:S(2)}, u32[]{:S(2)}) %collective-permute-start.18) | collective-permute-done | bytes 196640 | tf_op jit(solution)/shard_map/ppermute | solution.py:12
  322.9 9.1 %all_to_all.74 = f32[4,64,256]{2,1,0:T(8,128)S(1)} all-to-all(f32[4,64,256]{2,1,0:T(8,128)S(1)} %stack.104), channel_id=1, replica_groups=mesh['leaf'=128,'sep'=4] {'sep'}, dimensions={0} | all-to-all | bytes 524288 | tf_op jit(solution)/shard_map/all_to_all | solution.py:38
  336.5 2.5 collective-permute-done.19
  339.1 6.0 %collective-permute-done.20 = f32[64,4,256]{2,0,1:T(8,128)S(1)} collective-permute-done((f32[64,4,256]{2,0,1:T(8,128)S(1)}, f32[64,4,256]{2,0,1:T(8,128)S(1)}, u32[]{:S(2)}, u32[]{:S(2)}) %collective-permute-start.20) | collective-permute-done | bytes 262176 | tf_op jit(solution)/shard_map/ppermute | solution.py:12
  345.2 9.1 %all_to_all.75 = f32[4,64,256]{2,1,0:T(8,128)S(1)} all-to-all(f32[4,64,256]{2,1,0:T(8,128)S(1)} %stack.105), channel_id=1, replica_groups=mesh['leaf'=128,'sep'=4] {'sep'}, dimensions={0} | all-to-all | bytes 524288 | tf_op jit(solution)/shard_map/all_to_all | solution.py:38
  356.1 8.9 %collective-permute-start.21 = (f32[64,5,256]{2,0,1:T(8,128)S(1)}, f32[64,5,256]{2,0,1:T(8,128)S(1)}, u32[]{:S(2)}, u32[]{:S(2)}) collective-permute-start(f32[64,5,256]{2,0,1:T(8,128)S(1)} %slice.711), channel_id=1, source_target_pairs={{0,8},{4,12},{8,16},{12,20},{16,24},{20,28},{24,32},{28,36},{32,40... | collective-permute-start | bytes 983048 | tf_op jit(solution)/shard_map/ppermute | solution.py:12
  365.1 1.9 collective-permute-start.22
  367.0 2.6 collective-permute-done.21
  369.6 4.4 collective-permute-done.22
  374.2 9.1 %all_to_all.76 = f32[4,64,256]{2,1,0:T(8,128)S(1)} all-to-all(f32[4,64,256]{2,1,0:T(8,128)S(1)} %stack.106), channel_id=1, replica_groups=mesh['leaf'=128,'sep'=4] {'sep'}, dimensions={0} | all-to-all | bytes 524288 | tf_op jit(solution)/shard_map/all_to_all | solution.py:38
  385.2 1.9 collective-permute-start.23
  387.1 3.6 collective-permute-start.24
  390.8 3.5 collective-permute-done.23
  394.3 1.8 collective-permute-done.24
  396.3 9.8 %all_to_all.77 = f32[4,64,256]{2,1,0:T(8,128)S(1)} all-to-all(f32[4,64,256]{2,1,0:T(8,128)S(1)} %stack.107), channel_id=1, replica_groups=mesh['leaf'=128,'sep'=4] {'sep'}, dimensions={0} | all-to-all | bytes 524288 | tf_op jit(solution)/shard_map/all_to_all | solution.py:38
  407.3 1.9 collective-permute-start.25
  409.3 6.0 %collective-permute-done.25 = f32[64,7,256]{2,0,1:T(8,128)S(1)} collective-permute-done((f32[64,7,256]{2,0,1:T(8,128)S(1)}, f32[64,7,256]{2,0,1:T(8,128)S(1)}, u32[]{:S(2)}, u32[]{:S(2)}) %collective-permute-start.25) | collective-permute-done | bytes 458784 | tf_op jit(solution)/shard_map/ppermute | solution.py:12
  416.8 3.7 all-to-all-start.13
  420.9 24.3 %all-to-all-done.13 = f32[4,64,7,256]{3,1,2,0:T(8,128)S(1)} async-done(((f32[4,64,7,256]{3,1,2,0:T(8,128)}), f32[4,64,7,256]{3,1,2,0:T(8,128)S(1)}, u32[]{:S(2)}, u32[]{:S(2)}) %all-to-all-start.13) | async-done | bytes 1835040 | tf_op jit(solution)/shard_map/all_to_all | solution.py:38
  445.3 1.8 convolution_select_fusion
  451.5 21.1 %reduce-scatter.7.cloned.1.call-done = f32[160,256]{1,0:T(8,128)} async-done(((f32[640,256]{1,0:T(8,128)}), f32[160,256]{1,0:T(8,128)}) %reduce-scatter.7.cloned.1.call-update) | async-done | bytes 163856
  (152 shorter events, 54.3 us)
Async XLA Ops:
  7.2 16.1 %copy-start = (f32[1,896,160]{1,2,0:T(8,128)S(1)}, f32[1,896,160]{1,2,0:T(8,128)}, u32[]{:S(2)}) copy-start(f32[1,896,160]{1,2,0:T(8,128)} %param.64) | copy-start | bytes 1720324
  7.2 62.5 %reduce-scatter.5.cloned.1.call-start = ((), (), s32[]{:S(2)}) async-start(), calls=%async_computation.16 | async-start | bytes 2621440 | tf_op jit(solution)/shard_map/reduce_scatter | solution.py:80
  23.3 2.3 copy-start.10
  25.6 4.2 copy-start.8
  29.9 52.2 %copy-start.3 = (f32[1,64,256]{2,1,0:T(8,128)S(1)}, f32[1,64,256]{2,1,0:T(8,128)}, u32[]{:S(2)}) copy-start(f32[1,64,256]{2,1,0:T(8,128)} %param.67) | copy-start | bytes 196612
  29.9 63.0 %copy-start.1 = (f32[1,256,256]{2,1,0:T(8,128)S(1)}, f32[1,256,256]{2,1,0:T(8,128)}, u32[]{:S(2)}) copy-start(f32[1,256,256]{2,1,0:T(8,128)} %param.68) | copy-start | bytes 786436
  70.9 22.6 %copy-start.2 = (f32[1,256,256]{2,1,0:T(8,128)S(1)}, f32[1,256,256]{2,1,0:T(8,128)}, u32[]{:S(2)}) copy-start(f32[1,256,256]{2,1,0:T(8,128)} %param.69) | copy-start | bytes 786436
  70.9 9.9 %collective-permute-start = (f32[64,7,256]{2,0,1:T(8,128)S(1)}, f32[64,7,256]{2,0,1:T(8,128)S(1)}, u32[]{:S(2)}, u32[]{:S(2)}) collective-permute-start(f32[64,7,256]{2,0,1:T(8,128)S(1)} %copy.105), channel_id=1, source_target_pairs={{0,4},{4,8},{8,12},{12,16},{16,20},{20,24},{24,28},{28,32},{32,36}... | collective-permute-start | bytes 1376264 | tf_op jit(solution)/shard_map/ppermute | solution.py:12
  82.8 10.1 %all-to-all-start = ((f32[4,64,256]{2,1,0:T(8,128)}), f32[4,64,256]{2,1,0:T(8,128)S(1)}, u32[]{:S(2)}, u32[]{:S(2)}) async-start(f32[4,64,256]{2,1,0:T(8,128)} %stack.43), calls=%async_computation.1 | async-start | bytes 524288 | tf_op jit(solution)/shard_map/all_to_all | solution.py:38
  93.9 9.1 %collective-permute-start.1 = (f32[64,6,256]{2,0,1:T(8,128)S(1)}, f32[64,6,256]{2,0,1:T(8,128)S(1)}, u32[]{:S(2)}, u32[]{:S(2)}) collective-permute-start(f32[64,6,256]{2,0,1:T(8,128)S(1)} %slice.686), channel_id=1, source_target_pairs={{0,4},{4,8},{8,12},{12,16},{16,20},{20,24},{24,28},{28,32},{32,36}... | collective-permute-start | bytes 1179656 | tf_op jit(solution)/shard_map/ppermute | solution.py:12
  95.8 8.9 %collective-permute-start.2 = (f32[64,6,256]{2,0,1:T(8,128)S(1)}, f32[64,6,256]{2,0,1:T(8,128)S(1)}, u32[]{:S(2)}, u32[]{:S(2)}) collective-permute-start(f32[64,6,256]{2,0,1:T(8,128)S(1)} %slice.686), channel_id=1, source_target_pairs={{4,0},{8,4},{12,8},{16,12},{20,16},{24,20},{28,24},{32,28},{36,32}... | collective-permute-start | bytes 1179656 | tf_op jit(solution)/shard_map/ppermute | solution.py:12
  105.6 10.7 %all-to-all-start.1 = ((f32[4,64,256]{2,1,0:T(8,128)}), f32[4,64,256]{2,1,0:T(8,128)S(1)}, u32[]{:S(2)}, u32[]{:S(2)}) async-start(f32[4,64,256]{2,1,0:T(8,128)} %stack.45), calls=%async_computation.2 | async-start | bytes 524288 | tf_op jit(solution)/shard_map/all_to_all | solution.py:38
  117.3 12.1 %collective-permute-start.3 = (f32[64,5,256]{2,0,1:T(8,128)S(1)}, f32[64,5,256]{2,0,1:T(8,128)S(1)}, u32[]{:S(2)}, u32[]{:S(2)}) collective-permute-start(f32[64,5,256]{2,0,1:T(8,128)S(1)} %slice.689), channel_id=1, source_target_pairs={{0,8},{4,12},{8,16},{12,20},{16,24},{20,28},{24,32},{28,36},{32,40... | collective-permute-start | bytes 983048 | tf_op jit(solution)/shard_map/ppermute | solution.py:12
  120.1 10.5 %collective-permute-start.4 = (f32[64,5,256]{2,0,1:T(8,128)S(1)}, f32[64,5,256]{2,0,1:T(8,128)S(1)}, u32[]{:S(2)}, u32[]{:S(2)}) collective-permute-start(f32[64,5,256]{2,0,1:T(8,128)S(1)} %slice.689), channel_id=1, source_target_pairs={{8,0},{12,4},{16,8},{20,12},{24,16},{28,20},{32,24},{36,28},{40,32... | collective-permute-start | bytes 983048 | tf_op jit(solution)/shard_map/ppermute | solution.py:12
  131.4 10.4 %all-to-all-start.2 = ((f32[4,64,256]{2,1,0:T(8,128)}), f32[4,64,256]{2,1,0:T(8,128)S(1)}, u32[]{:S(2)}, u32[]{:S(2)}) async-start(f32[4,64,256]{2,1,0:T(8,128)} %stack.93), calls=%async_computation.3 | async-start | bytes 524288 | tf_op jit(solution)/shard_map/all_to_all | solution.py:38
  142.8 14.0 %collective-permute-start.5 = (f32[64,4,256]{2,0,1:T(8,128)S(1)}, f32[64,4,256]{2,0,1:T(8,128)S(1)}, u32[]{:S(2)}, u32[]{:S(2)}) collective-permute-start(f32[64,4,256]{2,0,1:T(8,128)S(1)} %slice.692), channel_id=1, source_target_pairs={{0,16},{4,20},{8,24},{12,28},{16,32},{20,36},{24,40},{28,44},{32,4... | collective-permute-start | bytes 786440 | tf_op jit(solution)/shard_map/ppermute | solution.py:12
  151.7 12.1 %collective-permute-start.6 = (f32[64,4,256]{2,0,1:T(8,128)S(1)}, f32[64,4,256]{2,0,1:T(8,128)}, u32[]{:S(2)}, u32[]{:S(2)}) collective-permute-start(f32[64,4,256]{2,0,1:T(8,128)S(1)} %slice.692), channel_id=1, source_target_pairs={{16,0},{20,4},{24,8},{28,12},{32,16},{36,20},{40,24},{44,28},{48,3... | collective-permute-start | bytes 786440 | tf_op jit(solution)/shard_map/ppermute | solution.py:12
  165.5 10.1 %all-to-all-start.3 = ((f32[4,64,256]{2,1,0:T(8,128)}), f32[4,64,256]{2,1,0:T(8,128)S(1)}, u32[]{:S(2)}, u32[]{:S(2)}) async-start(f32[4,64,256]{2,1,0:T(8,128)} %stack.95), calls=%async_computation.4 | async-start | bytes 524288 | tf_op jit(solution)/shard_map/all_to_all | solution.py:38
  176.6 10.2 %collective-permute-start.7 = (f32[64,3,256]{2,0,1:T(8,128)S(1)}, f32[64,3,256]{2,0,1:T(8,128)S(1)}, u32[]{:S(2)}, u32[]{:S(2)}) collective-permute-start(f32[64,3,256]{2,0,1:T(8,128)S(1)} %slice.695), channel_id=1, source_target_pairs={{0,32},{4,36},{8,40},{12,44},{16,48},{20,52},{24,56},{28,60},{32,6... | collective-permute-start | bytes 589832 | tf_op jit(solution)/shard_map/ppermute | solution.py:12
  183.5 17.7 %collective-permute-start.8 = (f32[64,3,256]{2,0,1:T(8,128)S(1)}, f32[64,3,256]{2,0,1:T(8,128)}, u32[]{:S(2)}, u32[]{:S(2)}) collective-permute-start(f32[64,3,256]{2,0,1:T(8,128)S(1)} %slice.695), channel_id=1, source_target_pairs={{32,0},{36,4},{40,8},{44,12},{48,16},{52,20},{56,24},{60,28},{64,3... | collective-permute-start | bytes 589832 | tf_op jit(solution)/shard_map/ppermute | solution.py:12
  202.9 10.1 %all-to-all-start.4 = ((f32[4,64,256]{2,1,0:T(8,128)}), f32[4,64,256]{2,1,0:T(8,128)S(1)}, u32[]{:S(2)}, u32[]{:S(2)}) async-start(f32[4,64,256]{2,1,0:T(8,128)} %stack.97), calls=%async_computation.5 | async-start | bytes 524288 | tf_op jit(solution)/shard_map/all_to_all | solution.py:38
  214.0 6.9 %collective-permute-start.10 = (f32[64,2,256]{2,0,1:T(8,128)S(1)}, f32[64,2,256]{2,0,1:T(8,128)S(1)}, u32[]{:S(2)}, u32[]{:S(2)}) collective-permute-start(f32[64,2,256]{2,0,1:T(8,128)S(1)} %slice.698), channel_id=1, source_target_pairs={{64,0},{68,4},{72,8},{76,12},{80,16},{84,20},{88,24},{92,28},{96,3... | collective-permute-start | bytes 393224 | tf_op jit(solution)/shard_map/ppermute | solution.py:12
  215.3 7.1 %collective-permute-start.9 = (f32[64,2,256]{2,0,1:T(8,128)S(1)}, f32[64,2,256]{2,0,1:T(8,128)S(1)}, u32[]{:S(2)}, u32[]{:S(2)}) collective-permute-start(f32[64,2,256]{2,0,1:T(8,128)S(1)} %slice.698), channel_id=1, source_target_pairs={{0,64},{4,68},{8,72},{12,76},{16,80},{20,84},{24,88},{28,92},{32,9... | collective-permute-start | bytes 393224 | tf_op jit(solution)/shard_map/ppermute | solution.py:12
  232.4 7.7 %collective-permute-start.11 = (f32[64,1,256]{2,0,1:T(8,128)S(1)}, f32[64,1,256]{2,0,1:T(8,128)S(1)}, u32[]{:S(2)}, u32[]{:S(2)}) collective-permute-start(f32[64,1,256]{2,0,1:T(8,128)S(1)} %slice_add_fusion), channel_id=1, source_target_pairs={{0,128},{4,132},{8,136},{12,140},{16,144},{20,148},{24,152},{28,15... | collective-permute-start | bytes 196616 | tf_op jit(solution)/shard_map/ppermute | solution.py:12
  238.3 10.4 %collective-permute-start.12 = (f32[64,1,256]{2,0,1:T(8,128)S(1)}, f32[64,1,256]{2,0,1:T(8,128)S(1)}, u32[]{:S(2)}, u32[]{:S(2)}) collective-permute-start(f32[64,1,256]{2,0,1:T(8,128)S(1)} %slice_add_fusion), channel_id=1, source_target_pairs={{128,0},{132,4},{136,8},{140,12},{144,16},{148,20},{152,24},{156,2... | collective-permute-start | bytes 196616 | tf_op jit(solution)/shard_map/ppermute | solution.py:12
  259.0 7.9 %collective-permute-start.13 = (f32[64,1,256]{2,0,1:T(8,128)S(1)}, f32[64,1,256]{2,0,1:T(8,128)S(1)}, u32[]{:S(2)}, u32[]{:S(2)}) collective-permute-start(f32[64,1,256]{2,0,1:T(8,128)S(1)} %select_bitcast_fusion), channel_id=1, source_target_pairs={{0,128},{4,132},{8,136},{12,140},{16,144},{20,148},{24,152},{28,15... | collective-permute-start | bytes 196616 | tf_op jit(solution)/shard_map/ppermute | solution.py:12
  265.0 7.1 %collective-permute-start.14 = (f32[64,1,256]{2,0,1:T(8,128)S(1)}, f32[64,1,256]{2,0,1:T(8,128)S(1)}, u32[]{:S(2)}, u32[]{:S(2)}) collective-permute-start(f32[64,1,256]{2,0,1:T(8,128)S(1)} %select_bitcast_fusion), channel_id=1, source_target_pairs={{128,0},{132,4},{136,8},{140,12},{144,16},{148,20},{152,24},{156,2... | collective-permute-start | bytes 196616 | tf_op jit(solution)/shard_map/ppermute | solution.py:12
  282.4 3.9 collective-permute-start.15
  283.8 7.1 %collective-permute-start.16 = (f32[64,2,256]{2,0,1:T(8,128)S(1)}, f32[64,2,256]{2,0,1:T(8,128)S(1)}, u32[]{:S(2)}, u32[]{:S(2)}) collective-permute-start(f32[64,2,256]{2,0,1:T(8,128)S(1)} %slice.702), channel_id=1, source_target_pairs={{64,0},{68,4},{72,8},{76,12},{80,16},{84,20},{88,24},{92,28},{96,3... | collective-permute-start | bytes 393224 | tf_op jit(solution)/shard_map/ppermute | solution.py:12
  301.4 10.8 %collective-permute-start.17 = (f32[64,3,256]{2,0,1:T(8,128)S(1)}, f32[64,3,256]{2,0,1:T(8,128)S(1)}, u32[]{:S(2)}, u32[]{:S(2)}) collective-permute-start(f32[64,3,256]{2,0,1:T(8,128)S(1)} %slice.705), channel_id=1, source_target_pairs={{0,32},{4,36},{8,40},{12,44},{16,48},{20,52},{24,56},{28,60},{32,6... | collective-permute-start | bytes 589832 | tf_op jit(solution)/shard_map/ppermute | solution.py:12
  308.5 14.3 %collective-permute-start.18 = (f32[64,3,256]{2,0,1:T(8,128)S(1)}, f32[64,3,256]{2,0,1:T(8,128)S(1)}, u32[]{:S(2)}, u32[]{:S(2)}) collective-permute-start(f32[64,3,256]{2,0,1:T(8,128)S(1)} %slice.705), channel_id=1, source_target_pairs={{32,0},{36,4},{40,8},{44,12},{48,16},{52,20},{56,24},{60,28},{64,3... | collective-permute-start | bytes 589832 | tf_op jit(solution)/shard_map/ppermute | solution.py:12
  333.9 5.2 %collective-permute-start.19 = (f32[64,4,256]{2,0,1:T(8,128)S(1)}, f32[64,4,256]{2,0,1:T(8,128)S(1)}, u32[]{:S(2)}, u32[]{:S(2)}) collective-permute-start(f32[64,4,256]{2,0,1:T(8,128)S(1)} %slice.708), channel_id=1, source_target_pairs={{0,16},{4,20},{8,24},{12,28},{16,32},{20,36},{24,40},{28,44},{32,4... | collective-permute-start | bytes 786440 | tf_op jit(solution)/shard_map/ppermute | solution.py:12
  335.2 9.8 %collective-permute-start.20 = (f32[64,4,256]{2,0,1:T(8,128)S(1)}, f32[64,4,256]{2,0,1:T(8,128)S(1)}, u32[]{:S(2)}, u32[]{:S(2)}) collective-permute-start(f32[64,4,256]{2,0,1:T(8,128)S(1)} %slice.708), channel_id=1, source_target_pairs={{16,0},{20,4},{24,8},{28,12},{32,16},{36,20},{40,24},{44,28},{48,3... | collective-permute-start | bytes 786440 | tf_op jit(solution)/shard_map/ppermute | solution.py:12
  356.1 13.5 %collective-permute-start.21 = (f32[64,5,256]{2,0,1:T(8,128)S(1)}, f32[64,5,256]{2,0,1:T(8,128)S(1)}, u32[]{:S(2)}, u32[]{:S(2)}) collective-permute-start(f32[64,5,256]{2,0,1:T(8,128)S(1)} %slice.711), channel_id=1, source_target_pairs={{0,8},{4,12},{8,16},{12,20},{16,24},{20,28},{24,32},{28,36},{32,40... | collective-permute-start | bytes 983048 | tf_op jit(solution)/shard_map/ppermute | solution.py:12
  365.1 9.0 %collective-permute-start.22 = (f32[64,5,256]{2,0,1:T(8,128)S(1)}, f32[64,5,256]{2,0,1:T(8,128)S(1)}, u32[]{:S(2)}, u32[]{:S(2)}) collective-permute-start(f32[64,5,256]{2,0,1:T(8,128)S(1)} %slice.711), channel_id=1, source_target_pairs={{8,0},{12,4},{16,8},{20,12},{24,16},{28,20},{32,24},{36,28},{40,32... | collective-permute-start | bytes 983048 | tf_op jit(solution)/shard_map/ppermute | solution.py:12
  385.2 9.1 %collective-permute-start.23 = (f32[64,6,256]{2,0,1:T(8,128)S(1)}, f32[64,6,256]{2,0,1:T(8,128)S(1)}, u32[]{:S(2)}, u32[]{:S(2)}) collective-permute-start(f32[64,6,256]{2,0,1:T(8,128)S(1)} %slice.714), channel_id=1, source_target_pairs={{0,4},{4,8},{8,12},{12,16},{16,20},{20,24},{24,28},{28,32},{32,36}... | collective-permute-start | bytes 1179656 | tf_op jit(solution)/shard_map/ppermute | solution.py:12
  387.1 8.9 %collective-permute-start.24 = (f32[64,6,256]{2,0,1:T(8,128)S(1)}, f32[64,6,256]{2,0,1:T(8,128)S(1)}, u32[]{:S(2)}, u32[]{:S(2)}) collective-permute-start(f32[64,6,256]{2,0,1:T(8,128)S(1)} %slice.714), channel_id=1, source_target_pairs={{4,0},{8,4},{12,8},{16,12},{20,16},{24,20},{28,24},{32,28},{36,32}... | collective-permute-start | bytes 1179656 | tf_op jit(solution)/shard_map/ppermute | solution.py:12
  407.3 7.9 %collective-permute-start.25 = (f32[64,7,256]{2,0,1:T(8,128)S(1)}, f32[64,7,256]{2,0,1:T(8,128)S(1)}, u32[]{:S(2)}, u32[]{:S(2)}) collective-permute-start(f32[64,7,256]{2,0,1:T(8,128)S(1)} %get-tuple-element.328), channel_id=1, source_target_pairs={{4,0},{8,4},{12,8},{16,12},{20,16},{24,20},{28,24},{32,28},{36,32}... | collective-permute-start | bytes 1376264 | tf_op jit(solution)/shard_map/ppermute | solution.py:12
  416.8 4.0 copy-start.11
  416.8 28.4 %all-to-all-start.13 = ((f32[4,64,7,256]{3,1,2,0:T(8,128)}), f32[4,64,7,256]{3,1,2,0:T(8,128)S(1)}, u32[]{:S(2)}, u32[]{:S(2)}) async-start(f32[4,64,7,256]{3,1,2,0:T(8,128)} %stack.108), calls=%async_computation.14 | async-start | bytes 3670016 | tf_op jit(solution)/shard_map/all_to_all | solution.py:38
  420.5 52.1 %reduce-scatter.7.cloned.1.call-start = ((), (), s32[]{:S(2)}) async-start(), calls=%async_computation.17 | async-start | bytes 819200
  420.9 24.4 %copy-start.9 = (s32[896]{0:T(1024)S(1)}, s32[896]{0:T(1024)}, u32[]{:S(2)}) copy-start(s32[896]{0:T(1024)} %copy-done.8) | copy-start | bytes 10756
  445.3 2.6 copy-start.4
  448.8 1.5 copy-start.5
  448.8 1.6 copy-start.6
  448.8 1.7 copy-start.7
Sparse Core Ops, SparseCore 0:
  30.0 39.6 reduce-scatter.4
  450.0 22.5 reduce-scatter.6
